TPU v7x, 32 devices: a whole 2x2x4 slice. The times are simulated.
32 devices in a mesh: freq: 2 (over y), harm: 4 (over z), wall: 4 (over x, core).
Axes of the slice: x: 2, y: 2, z: 4, core: 2. Of those that a mesh axis runs over, the one named last changes fastest.
Arguments:
- sketch: bfloat16 [32, 1024, 128], P(('freq', 'harm'), 'wall'), parts along dimension 0, may hold values from -48 to 48
- inverse_blocks: bfloat16 [32, 1024, 1024], P(('freq', 'harm'), 'wall'), parts along dimension 0, may hold values from -0.1875 to 0.1875
- couple_up: bfloat16 [8, 1024, 1024], P('freq', 'wall'), parts along dimension 0, may hold values from -0.03125 to 0.03125
- couple_down: bfloat16 [8, 1024, 1024], P('freq', 'wall'), parts along dimension 0, may hold values from -0.03125 to 0.03125
- strip_harmonics: int32 [8], P('freq'), parts along dimension 0, may hold values from 0 to 3
Outputs:
- basis: float32 [32, 1024, 128], P(('freq', 'harm'), 'wall'), parts along dimension 0
- triangle: float32 [256, 128], P('freq'), parts along dimension 0
There are 2 independent parts, one for each index of `freq`. A program takes and returns all parts, laid end to end along the dimension named above; each array names one. Nothing has to cross between parts.
Inputs may be any that keep to these rules, and one draw needn't show every extreme that they name: `strip_harmonics`: each entry one of 0 to 3; entries may repeat.
All inputs are finite; a program needn't handle non-finite values.
Results may differ from a plain program's by a relative error of at most 0.0045.
Values may be sent and summed in bfloat16 or wider, within the bound.
A program may use at most 64 MiB of HBM per device.

v0:
```python
import jax
import jax.numpy as jnp
from jax import lax
from jax.sharding import PartitionSpec as P

BAND = 4
SWEEPS = 3


def padded(cells, sides, width):
    for axis, dim in sides:
        count = lax.axis_size(axis)
        head = lax.slice_in_dim(cells, 0, width, axis=dim)
        tail = lax.slice_in_dim(cells, cells.shape[dim] - width, cells.shape[dim], axis=dim)
        cells = jnp.concatenate(
            [
                lax.ppermute(tail, axis, [(i, (i + 1) % count) for i in range(count)]),
                cells,
                lax.ppermute(head, axis, [((i + 1) % count, i) for i in range(count)]),
            ],
            axis=dim,
        )
    return cells


def body(sketch, inverse_blocks, couple_up, couple_down, strip_harmonics):
    offsets = strip_harmonics + 1
    local_count = sketch.shape[0]
    row_count = sketch.shape[1]
    width = sketch.shape[2]
    empty = jnp.zeros((local_count, row_count, width), jnp.float32)

    def add_inverse(piece):
        return jnp.einsum("hrc,hck->hrk", inverse_blocks, piece, preferred_element_type=jnp.float32)

    def apply_inverse(source):
        return add_inverse(lax.all_gather(source, "wall", axis=1, tiled=True))

    state = apply_inverse(sketch).astype(jnp.bfloat16)
    sampled = None
    for sweep in range(SWEEPS):
        extended = padded(state, (("harm", 0),), BAND)
        total = empty
        add_piece = lax.all_gather(extended, "wall", axis=1, tiled=True)
        for j in range(BAND):
            up_cols = couple_up[j]
            down_cols = couple_down[j]
            below = lax.dynamic_slice_in_dim(add_piece, BAND - offsets[j], local_count, 0)
            above = lax.dynamic_slice_in_dim(add_piece, BAND + offsets[j], local_count, 0)
            total = total + jnp.einsum(
                "rc,hck->hrk", up_cols, below, preferred_element_type=jnp.float32
            )
            total = total + jnp.einsum(
                "rc,hck->hrk", down_cols, above, preferred_element_type=jnp.float32
            )
        rhs = (sketch.astype(jnp.float32) - total).astype(jnp.bfloat16)
        result = apply_inverse(rhs)
        if sweep < SWEEPS - 1:
            state = result.astype(jnp.bfloat16)
        else:
            sampled = result
    flat = sampled.reshape(local_count * row_count, width)
    count = lax.axis_size("harm") * lax.axis_size("wall") * local_count * row_count
    local_gram = jnp.dot(
        flat.T, flat, precision=lax.Precision.HIGHEST, preferred_element_type=jnp.float32
    )
    gram = lax.psum(local_gram, ("harm", "wall")) / count
    lower = jnp.linalg.cholesky(gram)
    basis = jax.scipy.linalg.solve_triangular(lower, flat.T, lower=True).T
    triangle = lower.T
    return (basis.reshape(local_count, row_count, width), triangle)


def solution(mesh):
    return jax.shard_map(
        body,
        mesh=mesh,
        in_specs=(
            P(("freq", "harm"), "wall", None),
            P(("freq", "harm"), "wall", None),
            P("freq", "wall", None),
            P("freq", "wall", None),
            P("freq"),
        ),
        out_specs=(P(("freq", "harm"), "wall", None), P("freq", None)),
        check_vma=False,
    )
```

profile of v0, /device:TPU:0, one launch (start us, length us, event | category | flops | bytes accessed | tf_op | source)
XLA Modules:
  0.0 369.7 jit_solution(4480394632407928866)
XLA Ops:
  8.0 21.0 %all-gather.8.cloned.1.call-done = bf16[4,1024,128]{2,1,0:T(8,128)(2,1)} async-done(((bf16[4,256,128]{2,1,0:T(8,128)(2,1)}), bf16[4,1024,128]{2,1,0:T(8,128)(2,1)}) %all-gather.8.cloned.1.call-update) | async-done | bytes 1048592 | tf_op jit(solution)/shard_map/all_gather | solution.py:37
  31.0 3.4 collective-permute-start.1
  34.3 6.7 %collective-permute-done.1 = bf16[4,256,128]{2,1,0:T(8,128)(2,1)S(1)} collective-permute-done((bf16[4,256,128]{2,1,0:T(8,128)(2,1)S(1)}, bf16[4,256,128]{2,1,0:T(8,128)(2,1)S(1)}, u32[]{:S(2)}, u32[]{:S(2)}) %collective-permute-start.1) | collective-permute-done | bytes 262176 | tf_op jit(solution)/shard_map/ppermute | solution.py:19
  41.1 5.8 %collective-permute-done = bf16[4,256,128]{2,1,0:T(8,128)(2,1)S(1)} collective-permute-done((bf16[4,256,128]{2,1,0:T(8,128)(2,1)S(1)}, bf16[4,256,128]{2,1,0:T(8,128)(2,1)S(1)}, u32[]{:S(2)}, u32[]{:S(2)}) %collective-permute-start) | collective-permute-done | bytes 262176 | tf_op jit(solution)/shard_map/ppermute | solution.py:17
  58.8 16.2 %all-gather.10.cloned.1.call-done = bf16[12,1024,128]{2,1,0:T(8,128)(2,1)} async-done(((bf16[12,256,128]{2,1,0:T(8,128)(2,1)}), bf16[12,1024,128]{2,1,0:T(8,128)(2,1)}) %all-gather.10.cloned.1.call-update) | async-done | bytes 3145744 | tf_op jit(solution)/shard_map/all_gather | solution.py:44
  75.0 2.0 fusion.35
  83.9 16.9 %all-gather.12.cloned.1.call-done = bf16[4,1024,128]{1,2,0:T(8,128)(2,1)} async-done(((bf16[4,256,128]{1,2,0:T(8,128)(2,1)}), bf16[4,1024,128]{1,2,0:T(8,128)(2,1)}) %all-gather.12.cloned.1.call-update) | async-done | bytes 1048592 | tf_op jit(solution)/shard_map/all_gather | solution.py:37
  100.8 2.1 fusion.9
  102.9 3.4 collective-permute-start.3
  106.3 6.7 %collective-permute-done.3 = bf16[4,256,128]{1,2,0:T(8,128)(2,1)S(1)} collective-permute-done((bf16[4,256,128]{1,2,0:T(8,128)(2,1)S(1)}, bf16[4,256,128]{1,2,0:T(8,128)(2,1)S(1)}, u32[]{:S(2)}, u32[]{:S(2)}) %collective-permute-start.3) | collective-permute-done | bytes 262176 | tf_op jit(solution)/shard_map/ppermute | solution.py:19
  113.0 5.8 %collective-permute-done.2 = bf16[4,256,128]{1,2,0:T(8,128)(2,1)S(1)} collective-permute-done((bf16[4,256,128]{1,2,0:T(8,128)(2,1)S(1)}, bf16[4,256,128]{1,2,0:T(8,128)(2,1)S(1)}, u32[]{:S(2)}, u32[]{:S(2)}) %collective-permute-start.2) | collective-permute-done | bytes 262176 | tf_op jit(solution)/shard_map/ppermute | solution.py:17
  119.9 27.4 %all-gather.14.cloned.1.call-done = bf16[12,1024,128]{1,2,0:T(8,128)(2,1)} async-done(((bf16[12,256,128]{1,2,0:T(8,128)(2,1)}), bf16[12,1024,128]{1,2,0:T(8,128)(2,1)}) %all-gather.14.cloned.1.call-update) | async-done | bytes 3145744 | tf_op jit(solution)/shard_map/all_gather | solution.py:44
  147.3 2.0 fusion.26
  156.2 16.9 %all-gather.16.cloned.1.call-done = bf16[4,1024,128]{1,2,0:T(8,128)(2,1)} async-done(((bf16[4,256,128]{1,2,0:T(8,128)(2,1)}), bf16[4,1024,128]{1,2,0:T(8,128)(2,1)}) %all-gather.16.cloned.1.call-update) | async-done | bytes 1048592 | tf_op jit(solution)/shard_map/all_gather | solution.py:37
  173.1 2.1 fusion.10
  175.2 3.4 collective-permute-start.5
  178.6 6.7 %collective-permute-done.5 = bf16[4,256,128]{1,2,0:T(8,128)(2,1)S(1)} collective-permute-done((bf16[4,256,128]{1,2,0:T(8,128)(2,1)S(1)}, bf16[4,256,128]{1,2,0:T(8,128)(2,1)S(1)}, u32[]{:S(2)}, u32[]{:S(2)}) %collective-permute-start.5) | collective-permute-done | bytes 262176 | tf_op jit(solution)/shard_map/ppermute | solution.py:19
  185.3 5.8 %collective-permute-done.4 = bf16[4,256,128]{1,2,0:T(8,128)(2,1)S(1)} collective-permute-done((bf16[4,256,128]{1,2,0:T(8,128)(2,1)S(1)}, bf16[4,256,128]{1,2,0:T(8,128)(2,1)S(1)}, u32[]{:S(2)}, u32[]{:S(2)}) %collective-permute-start.4) | collective-permute-done | bytes 262176 | tf_op jit(solution)/shard_map/ppermute | solution.py:17
  192.4 27.2 %all-gather.18.cloned.1.call-done = bf16[12,1024,128]{1,2,0:T(8,128)(2,1)} async-done(((bf16[12,256,128]{1,2,0:T(8,128)(2,1)}), bf16[12,1024,128]{1,2,0:T(8,128)(2,1)}) %all-gather.18.cloned.1.call-update) | async-done | bytes 3145744 | tf_op jit(solution)/shard_map/all_gather | solution.py:44
  228.5 16.9 %all-gather.20.cloned.1.call-done = bf16[4,1024,128]{1,2,0:T(8,128)(2,1)} async-done(((bf16[4,256,128]{1,2,0:T(8,128)(2,1)}), bf16[4,1024,128]{1,2,0:T(8,128)(2,1)}) %all-gather.20.cloned.1.call-update) | async-done | bytes 1048592 | tf_op jit(solution)/shard_map/all_gather | solution.py:37
  245.4 2.1 convolution_bitcast_fusion
  248.7 87.0 %all-reduce.2.cloned.1.call-done = f32[128,128]{0,1:T(8,128)} async-done(((f32[128,128]{0,1:T(8,128)}), f32[128,128]{0,1:T(8,128)}) %all-reduce.2.cloned.1.call-update) | async-done | bytes 65552 | tf_op jit(solution)/shard_map/psum | solution.py:67
  337.5 11.7 %cholesky.16 = f32[128,128]{1,0:T(8,128)S(1)} custom-call(f32[128,128]{1,0:T(8,128)S(1)} %fusion.88), custom_call_target="Cholesky" | custom-call | tf_op jit(solution)/shard_map/jit(cholesky)/cholesky | solution.py:68
  351.3 9.8 %custom-call.7 = f32[1,128,128]{1,2,0:T(8,128)S(1)} custom-call(f32[1,128,128]{2,1,0:T(8,128)S(1)} %get-tuple-element.5), custom_call_target="InvertDiagBlocksLowerTriangular" | custom-call | tf_op jit(solution)/shard_map/jit(_solve_triangular)/triangular_solve | solution.py:69
  (81 shorter events, 36.1 us)
Async XLA Ops:
  7.2 21.8 %copy-start = (bf16[4,256,1024]{2,1,0:T(8,128)(2,1)S(1)}, bf16[4,256,1024]{2,1,0:T(8,128)(2,1)}, u32[]{:S(2)}) copy-start(bf16[4,256,1024]{2,1,0:T(8,128)(2,1)} %param.6) | copy-start | bytes 6291460
  7.2 21.8 %all-gather.8.cloned.1.call-start = ((), (), s32[]{:S(2)}) async-start(), calls=%async_computation | async-start | bytes 1310720 | tf_op jit(solution)/shard_map/all_gather | solution.py:37
  7.9 67.1 %all-gather.10.cloned.1.call-start = ((), (), s32[]{:S(2)}) async-start(), calls=%async_computation.1 | async-start | bytes 3932160 | tf_op jit(solution)/shard_map/all_gather | solution.py:44
  30.9 17.0 %copy-start.11 = (s32[4]{0:T(128)S(1)}, s32[4]{0:T(128)}, u32[]{:S(2)}) copy-start(s32[4]{0:T(128)} %param.9) | copy-start | bytes 52
  30.9 27.6 %copy-start.10 = (bf16[4,256,128]{2,1,0:T(8,128)(2,1)S(1)}, bf16[4,256,128]{2,1,0:T(8,128)(2,1)}, u32[]{:S(2)}) copy-start(bf16[4,256,128]{2,1,0:T(8,128)(2,1)} %param.5) | copy-start | bytes 786436
  31.0 10.1 %collective-permute-start.1 = (bf16[4,256,128]{2,1,0:T(8,128)(2,1)S(1)}, bf16[4,256,128]{2,1,0:T(8,128)(2,1)S(1)}, u32[]{:S(2)}, u32[]{:S(2)}) collective-permute-start(bf16[4,256,128]{2,1,0:T(8,128)(2,1)S(1)} %convolution_convert_fusion.2), channel_id=1, source_target_pairs={{4,0},{8,4},{12,8},{0,12},{5,1},{9,5},{13,9},{1,13},{6,2},{10,6},{... | collective-permute-start | bytes 786440 | tf_op jit(solution)/shard_map/ppermute | solution.py:19
  34.3 12.6 %collective-permute-start = (bf16[4,256,128]{2,1,0:T(8,128)(2,1)S(1)}, bf16[4,256,128]{2,1,0:T(8,128)(2,1)S(1)}, u32[]{:S(2)}, u32[]{:S(2)}) collective-permute-start(bf16[4,256,128]{2,1,0:T(8,128)(2,1)S(1)} %convolution_convert_fusion.2), channel_id=1, source_target_pairs={{0,4},{4,8},{8,12},{12,0},{1,5},{5,9},{9,13},{13,1},{2,6},{6,10},{... | collective-permute-start | bytes 786440 | tf_op jit(solution)/shard_map/ppermute | solution.py:17
  47.9 52.9 %all-gather.12.cloned.1.call-start = ((), (), s32[]{:S(2)}) async-start(), calls=%async_computation.2 | async-start | bytes 1310720 | tf_op jit(solution)/shard_map/all_gather | solution.py:37
  77.0 3.6 copy-start.4
  77.0 3.6 copy-start.7
  83.9 63.5 %all-gather.14.cloned.1.call-start = ((), (), s32[]{:S(2)}) async-start(), calls=%async_computation.3 | async-start | bytes 3932160 | tf_op jit(solution)/shard_map/all_gather | solution.py:44
  102.9 10.1 %collective-permute-start.3 = (bf16[4,256,128]{1,2,0:T(8,128)(2,1)S(1)}, bf16[4,256,128]{1,2,0:T(8,128)(2,1)S(1)}, u32[]{:S(2)}, u32[]{:S(2)}) collective-permute-start(bf16[4,256,128]{1,2,0:T(8,128)(2,1)S(1)} %fusion.9), channel_id=1, source_target_pairs={{4,0},{8,4},{12,8},{0,12},{5,1},{9,5},{13,9},{1,13},{6,2},{10,6},{... | collective-permute-start | bytes 786440 | tf_op jit(solution)/shard_map/ppermute | solution.py:19
  106.3 12.6 %collective-permute-start.2 = (bf16[4,256,128]{1,2,0:T(8,128)(2,1)S(1)}, bf16[4,256,128]{1,2,0:T(8,128)(2,1)S(1)}, u32[]{:S(2)}, u32[]{:S(2)}) collective-permute-start(bf16[4,256,128]{1,2,0:T(8,128)(2,1)S(1)} %fusion.9), channel_id=1, source_target_pairs={{0,4},{4,8},{8,12},{12,0},{1,5},{5,9},{9,13},{13,1},{2,6},{6,10},{... | collective-permute-start | bytes 786440 | tf_op jit(solution)/shard_map/ppermute | solution.py:17
  119.9 53.3 %all-gather.16.cloned.1.call-start = ((), (), s32[]{:S(2)}) async-start(), calls=%async_computation.4 | async-start | bytes 1310720 | tf_op jit(solution)/shard_map/all_gather | solution.py:37
  147.3 2.1 copy-start.2
  149.4 3.6 copy-start.6
  149.4 3.6 copy-start.8
  156.2 63.5 %all-gather.18.cloned.1.call-start = ((), (), s32[]{:S(2)}) async-start(), calls=%async_computation.5 | async-start | bytes 3932160 | tf_op jit(solution)/shard_map/all_gather | solution.py:44
  175.2 10.1 %collective-permute-start.5 = (bf16[4,256,128]{1,2,0:T(8,128)(2,1)S(1)}, bf16[4,256,128]{1,2,0:T(8,128)(2,1)S(1)}, u32[]{:S(2)}, u32[]{:S(2)}) collective-permute-start(bf16[4,256,128]{1,2,0:T(8,128)(2,1)S(1)} %fusion.10), channel_id=1, source_target_pairs={{4,0},{8,4},{12,8},{0,12},{5,1},{9,5},{13,9},{1,13},{6,2},{10,6},{... | collective-permute-start | bytes 786440 | tf_op jit(solution)/shard_map/ppermute | solution.py:19
  178.6 12.6 %collective-permute-start.4 = (bf16[4,256,128]{1,2,0:T(8,128)(2,1)S(1)}, bf16[4,256,128]{1,2,0:T(8,128)(2,1)S(1)}, u32[]{:S(2)}, u32[]{:S(2)}) collective-permute-start(bf16[4,256,128]{1,2,0:T(8,128)(2,1)S(1)} %fusion.10), channel_id=1, source_target_pairs={{0,4},{4,8},{8,12},{12,0},{1,5},{5,9},{9,13},{13,1},{2,6},{6,10},{... | collective-permute-start | bytes 786440 | tf_op jit(solution)/shard_map/ppermute | solution.py:17
  192.2 53.3 %all-gather.20.cloned.1.call-start = ((), (), s32[]{:S(2)}) async-start(), calls=%async_computation.6 | async-start | bytes 1310720 | tf_op jit(solution)/shard_map/all_gather | solution.py:37
  221.7 3.6 copy-start.5
  221.7 3.6 copy-start.9
  228.5 107.2 %all-reduce.2.cloned.1.call-start = ((), (), s32[]{:S(2)}) async-start(), calls=%async_computation.7 | async-start | bytes 131072 | tf_op jit(solution)/shard_map/psum | solution.py:67
  (2 other events, 4.1 us)
Sparse Core Ops, SparseCore 0:
  9.5 19.4 all-gather.7
  48.0 26.9 all-gather.9
  84.0 16.8 all-gather.11
  120.0 27.3 all-gather.13
  156.3 16.8 all-gather.15
  192.3 27.3 all-gather.17
  228.6 16.8 all-gather.19
  249.5 86.1 all-reduce.1
where the time goes:
time: 371 us; the launch traced here: 370 us
  waiting for transfers between devices  268 us (72%)
  matrix products  37.1 us (10%)
  other arithmetic  27.5 us (7%)
  between operations  24.5 us (7%)
  starting transfers between devices  10.7 us (3%)
    psum x1, waiting for transfers between devices, body(): gram = lax.psum(local_gram, ('harm', 'wall')) / count  87 us
    all_gather x4, waiting for transfers between devices, apply_inverse(): return add_inverse(lax.all_gather(source, 'wall', axis=1, tiled=True))  71.8 us
    all_gather x3, waiting for transfers between devices, body(): add_piece = lax.all_gather(extended, 'wall', axis=1, tiled=True)  70.8 us
    ppermute x3, waiting for transfers between devices, padded(): lax.ppermute(head, axis, [((i + 1) % count, i) for i in range(count)])  20.2 us
    ppermute x3, waiting for transfers between devices, padded(): lax.ppermute(tail, axis, [(i, (i + 1) % count) for i in range(count)])  17.5 us
    dot_general x12, matrix products, body(): jnp.einsum('rc,hck->hrk', up_cols, below, preferred_element_type=jnp.floa...  13.6 us
    dot_general x12, matrix products, body(): jnp.einsum('rc,hck->hrk', down_cols, above, preferred_element_type=jnp.fl...  12.4 us
    another operation x3, other arithmetic, body(): lower = jnp.linalg.cholesky(gram)  12.4 us
  transfers between devices with their start and end apart: 14, of which 14 were waited for; matrix products, arithmetic and copies ran while one was open for 0% of the time, Pallas kernels for 0%

commit v1 on v0

v1 whole, which is shorter than its diff:
```python
import functools

import jax
import jax.numpy as jnp
from jax import lax
from jax.experimental import pallas as pl
from jax.experimental.pallas import tpu as pltpu
from jax.sharding import PartitionSpec as P

BAND = 4
SWEEPS = 3
MESH = pl.DeviceIdType.MESH


def flip(index, bit):
    return index + bit - 2 * bit * (lax.div(index, bit) % 2)


def bits_of(count):
    return [1 << b for b in range(count.bit_length() - 1)]


def visit_order(count):
    order = []
    for i in range((count + 1) // 2):
        order += [i] if count - 1 - i == i else [i, count - 1 - i]
    return order


def sweep_kernel(
    walls, harms, strip, sketch, inverse, up, down, sampled, gram,
    pieces, inverse_v, couple_v, products, partial, halo_out, halo_in, gram_out, gram_in,
    load_sem, recv_sem, send_sem, halo_send, halo_recv, gram_send, gram_recv,
):
    count, rows, width = sketch.shape
    w = lax.axis_index("wall")
    z = lax.axis_index("harm")
    prev, following = (z + harms - 1) % harms, (z + 1) % harms
    wall_bits, harm_bits = bits_of(walls), bits_of(harms)
    order = visit_order(count)

    greet = [{"wall": flip(w, b)} for b in wall_bits]
    greet += [{"harm": flip(z, b)} for b in harm_bits]
    greet += [{"harm": prev}, {"harm": following}]
    barrier = pltpu.get_barrier_semaphore()

    loads = [
        pltpu.make_async_copy(inverse.at[h], inverse_v.at[h], load_sem.at[h]) for h in order
    ]
    loads += [
        pltpu.make_async_copy(up, couple_v.at[pl.ds(0, BAND)], load_sem.at[count]),
        pltpu.make_async_copy(down, couple_v.at[pl.ds(BAND, BAND)], load_sem.at[count + 1]),
    ]

    def block(g, h, m):
        source = w
        for b in wall_bits:
            if m & b:
                source = flip(source, b)
        return pieces.at[g, h, pl.ds(pl.multiple_of(source * rows, rows), rows)]

    own_copies = [
        pltpu.make_async_copy(sketch.at[h], block(0, h, 0), load_sem.at[count + 2 + h])
        for h in range(count)
    ]
    for copy in own_copies:
        copy.start()
    for peer in greet:
        pl.semaphore_signal(barrier, inc=1, device_id=peer, device_id_type=MESH)
    for copy in loads:
        copy.start()
    pl.semaphore_wait(barrier, len(greet))

    def hop(g, h, m, bit):
        return pltpu.make_async_remote_copy(
            src_ref=block(g, h, m), dst_ref=block(g, h, m),
            send_sem=send_sem.at[h, m + bit], recv_sem=recv_sem.at[g, h, m + bit],
            device_id={"wall": flip(w, bit)}, device_id_type=MESH,
        )

    def arrival(g, h, m):
        low = m & -m
        return pltpu.make_async_remote_copy(
            src_ref=block(g, h, m), dst_ref=block(g, h, m),
            send_sem=send_sem.at[h, m], recv_sem=recv_sem.at[g, h, m],
            device_id={"wall": flip(w, low)}, device_id_type=MESH,
        )

    def send_own(g, h):
        for bit in reversed(wall_bits):
            hop(g, h, 0, bit).start()

    def collect(g, h):
        for m in sorted(range(1, walls), key=lambda m: -(m & -m)):
            arrival(g, h, m).wait_recv()
            for bit in reversed(wall_bits):
                if bit < (m & -m):
                    hop(g, h, m, bit).start()

    def settle(g, h):
        for m in range(1, walls):
            arrival(g, h, m).wait_send()

    def apply_inverse(g, h):
        return jnp.dot(inverse_v[h], pieces[g, h], preferred_element_type=jnp.float32)

    def store_own(g, h, value):
        pieces[g, h, pl.ds(pl.multiple_of(w * rows, rows), rows), :] = value

    for h in order:
        own_copies[h].wait()
        send_own(0, h)

    blank = jnp.zeros((rows, width), jnp.float32)

    @pl.loop(0, 2 * BAND)
    def _(j):
        for slot in range(BAND):
            products[j, slot] = blank
            products[j, count + BAND + slot] = blank

    for i, h in enumerate(order):
        collect(0, h)
        loads[i].wait()
        state = apply_inverse(0, h).astype(jnp.bfloat16)
        settle(0, h)
        store_own(1, h, state)
        send_own(1, h)
    loads[count].wait()
    loads[count + 1].wait()

    offsets = [strip[j] + 1 for j in range(BAND)]

    def halo(s, side, i):
        return pltpu.make_async_remote_copy(
            src_ref=halo_out.at[s, side, i], dst_ref=halo_in.at[s, side, i],
            send_sem=halo_send.at[side, i], recv_sem=halo_recv.at[s, side, i],
            device_id={"harm": prev if side == 0 else following}, device_id_type=MESH,
        )

    def from_below(t):
        total = products[0, t - offsets[0] + BAND]
        for j in range(1, BAND):
            total = total + products[j, t - offsets[j] + BAND]
        return total

    def from_above(t):
        total = products[BAND, t + offsets[0] + BAND]
        for j in range(1, BAND):
            total = total + products[BAND + j, t + offsets[j] + BAND]
        return total

    slots = []
    for i in range(BAND):
        slots.append((1, i, {count + i - o for o in range(1, BAND + 1)}))
        slots.append((0, BAND - 1 - i, {o - 1 - i for o in range(1, BAND + 1)}))
    slots = [(side, i, {h for h in need if 0 <= h < count}) for side, i, need in slots]

    for s in range(SWEEPS):
        g_state, g_rhs = 1 + 2 * s, 2 + 2 * s
        done, sent = set(), set()
        for h in order:
            collect(g_state, h)

            @pl.loop(0, 2 * BAND)
            def _(j):
                products[j, h + BAND] = jnp.dot(
                    couple_v[j], pieces[g_state, h], preferred_element_type=jnp.float32
                )

            done.add(h)
            for side, i, need in slots:
                if (side, i) not in sent and need <= done:
                    sent.add((side, i))
                    value = from_above(i - BAND) if side == 0 else from_below(count + i)
                    halo_out[s, side, i] = value.astype(jnp.bfloat16)
                    halo(s, side, i).start()
        for h in order:
            settle(g_state, h)
            own = pieces[0, h, pl.ds(pl.multiple_of(w * rows, rows), rows), :]
            partial[h] = own.astype(jnp.float32) - (from_below(h) + from_above(h))
        for h in order:
            rhs = partial[h]
            if h < BAND:
                halo(s, 1, h).wait_recv()
                rhs = rhs - halo_in[s, 1, h].astype(jnp.float32)
            if h >= count - BAND:
                i = h - count + BAND
                halo(s, 0, i).wait_recv()
                rhs = rhs - halo_in[s, 0, i].astype(jnp.float32)
            store_own(g_rhs, h, rhs.astype(jnp.bfloat16))
            send_own(g_rhs, h)
        for side in range(2):
            for i in range(BAND):
                halo(s, side, i).wait_send()
        total = jnp.zeros((width, width), jnp.float32)
        for h in order:
            collect(g_rhs, h)
            result = apply_inverse(g_rhs, h)
            settle(g_rhs, h)
            if s < SWEEPS - 1:
                store_own(g_rhs + 1, h, result.astype(jnp.bfloat16))
                send_own(g_rhs + 1, h)
            else:
                sampled[h] = result
                total = total + lax.dot_general(
                    result, result, (((0,), (0,)), ((), ())),
                    precision=lax.Precision.HIGHEST, preferred_element_type=jnp.float32,
                )

    stages = [("wall", flip(w, b)) for b in wall_bits] + [("harm", flip(z, b)) for b in harm_bits]
    for stage, (axis, peer) in enumerate(stages):
        gram_out[stage] = total
        swap = pltpu.make_async_remote_copy(
            src_ref=gram_out.at[stage], dst_ref=gram_in.at[stage],
            send_sem=gram_send.at[stage], recv_sem=gram_recv.at[stage],
            device_id={axis: peer}, device_id_type=MESH,
        )
        swap.start()
        swap.wait()
        total = total + gram_in[stage]
    gram[...] = total / (harms * walls * count * rows)


def factor_kernel(sampled, gram, basis, triangle, work, inverse_lower):
    count, rows, width = sampled.shape
    row_at = lax.broadcasted_iota(jnp.int32, (width, width), 0)
    col_at = lax.broadcasted_iota(jnp.int32, (width, width), 1)
    work[...] = gram[...]
    inverse_lower[...] = jnp.where(row_at == col_at, 1.0, 0.0)

    @pl.loop(0, width)
    def _(k):
        a = work[...]
        x = inverse_lower[...]
        row = work[pl.ds(k, 1), :]
        x_row = inverse_lower[pl.ds(k, 1), :]
        column = jnp.sum(jnp.where(col_at == k, a, 0.0), axis=1, keepdims=True)
        pivot = jnp.sum(jnp.where(col_at[:1] == k, row, 0.0), axis=1, keepdims=True)
        unit = lax.rsqrt(pivot)
        factor = jnp.where(row_at[:, :1] > k, column / pivot, 0.0)
        here = row_at == k
        work[...] = jnp.where(here, row * unit, a - factor * row)
        inverse_lower[...] = jnp.where(here, x_row * unit, x - factor * x_row)

    triangle[...] = jnp.where(row_at <= col_at, work[...], 0.0)
    for h in range(count):
        basis[h] = lax.dot_general(
            sampled[h], inverse_lower[...], (((1,), (1,)), ((), ())),
            precision=lax.Precision.HIGHEST, preferred_element_type=jnp.float32,
        )


def body(walls, harms, sketch, inverse_blocks, couple_up, couple_down, strip_harmonics):
    count, rows, width = sketch.shape
    size = rows * walls
    wall_hops, stages = len(bits_of(walls)), len(bits_of(walls)) + len(bits_of(harms))
    gathers = 1 + 2 * SWEEPS
    vmem = pl.BlockSpec(memory_space=pltpu.VMEM)
    anywhere = pl.BlockSpec(memory_space=pl.ANY)
    sampled, gram = pl.pallas_call(
        functools.partial(sweep_kernel, walls, harms),
        out_shape=(
            jax.ShapeDtypeStruct((count, rows, width), jnp.float32),
            jax.ShapeDtypeStruct((width, width), jnp.float32),
        ),
        in_specs=[pl.BlockSpec(memory_space=pltpu.SMEM)] + [anywhere] * 4,
        out_specs=(vmem, vmem),
        scratch_shapes=[
            pltpu.VMEM((gathers, count, size, width), jnp.bfloat16),
            pltpu.VMEM((count, rows, size), jnp.bfloat16),
            pltpu.VMEM((2 * BAND, rows, size), jnp.bfloat16),
            pltpu.VMEM((2 * BAND, count + 2 * BAND, rows, width), jnp.float32),
            pltpu.VMEM((count, rows, width), jnp.float32),
            pltpu.VMEM((SWEEPS, 2, BAND, rows, width), jnp.bfloat16),
            pltpu.VMEM((SWEEPS, 2, BAND, rows, width), jnp.bfloat16),
            pltpu.VMEM((stages, width, width), jnp.float32),
            pltpu.VMEM((stages, width, width), jnp.float32),
            pltpu.SemaphoreType.DMA((2 * count + 2,)),
            pltpu.SemaphoreType.DMA((gathers, count, walls)),
            pltpu.SemaphoreType.DMA((count, walls)),
            pltpu.SemaphoreType.DMA((2, BAND)),
            pltpu.SemaphoreType.DMA((SWEEPS, 2, BAND)),
            pltpu.SemaphoreType.DMA((stages,)),
            pltpu.SemaphoreType.DMA((stages,)),
        ],
        compiler_params=pltpu.CompilerParams(
            collective_id=0, has_side_effects=True, vmem_limit_bytes=48 * 1024 * 1024
        ),
        name="sweeps",
    )(strip_harmonics, sketch, inverse_blocks, couple_up, couple_down)
    return pl.pallas_call(
        factor_kernel,
        out_shape=(
            jax.ShapeDtypeStruct((count, rows, width), jnp.float32),
            jax.ShapeDtypeStruct((width, width), jnp.float32),
        ),
        in_specs=[vmem, vmem],
        out_specs=(vmem, vmem),
        scratch_shapes=[pltpu.VMEM((width, width), jnp.float32)] * 2,
        name="factor",
    )(sampled, gram)


def solution(mesh):
    return jax.shard_map(
        functools.partial(body, mesh.shape["wall"], mesh.shape["harm"]),
        mesh=mesh,
        in_specs=(
            P(("freq", "harm"), "wall", None),
            P(("freq", "harm"), "wall", None),
            P("freq", "wall", None),
            P("freq", "wall", None),
            P("freq"),
        ),
        out_specs=(P(("freq", "harm"), "wall", None), P("freq", None)),
        check_vma=False,
    )
```

time: 371 us -> 138 us (0.37)
  waiting for transfers between devices: 268 us -> 0 us
  Pallas kernels: 0 us -> 131 us
  matrix products: 37.1 us -> 0 us
  other arithmetic: 27.5 us -> 0 us
  between operations: 24.5 us -> 0.66 us
  starting transfers between devices: 10.7 us -> 0 us
  local copies, waits for them, and re-layouts: 1.89 us -> 6.19 us
    all_gather x7 -> x0, waiting for transfers between devices: 143 us -> none  [the longest x4 71.8 us: apply_inverse(): return add_inverse(lax.all_gather(source, 'wall', axis=1, tiled=True))]
    pallas_call x0 -> x2, Pallas kernels: none -> 131 us  [the longest x1 114 us: body(): pl.pallas_call(functools.partial(sweep_kernel, walls, harms), out_shape=(...]
    psum x1 -> x0, waiting for transfers between devices: 87 us -> none  [body(): gram = lax.psum(local_gram, ('harm', 'wall')) / count]
    ppermute x6 -> x0, waiting for transfers between devices: 37.7 us -> none  [the longest x3 20.2 us: padded(): lax.ppermute(head, axis, [((i + 1) % count, i) for i in range(count)])]
    dot_general x29 -> x0, matrix products: 35.3 us -> none  [the longest x12 13.6 us: body(): jnp.einsum('rc,hck->hrk', up_cols, below, preferred_element_type=jnp.floa...]
    another operation x4 -> x0, other arithmetic: 22.2 us -> none  [the longest x3 12.4 us: body(): lower = jnp.linalg.cholesky(gram)]
    ppermute x6 -> x0, starting transfers between devices: 10.2 us -> none  [the longest x3 10.1 us: padded(): lax.ppermute(head, axis, [((i + 1) % count, i) for i in range(count)])]
    unnamed x26 -> x12, local copies, waits for them, and re-layouts: 1.14 us -> 6.19 us
  transfers between devices with their start and end apart: 14 -> 0, of which waited for: 14 -> 0; matrix products, arithmetic and copies ran while one was open for 0% -> 0% of each run, Pallas kernels for 0% -> 0%
where the time goes in v1:
time: 138 us; the launch traced here: 137 us
  Pallas kernels  131 us (95%)
  local copies, waits for them, and re-layouts  6.19 us (4%)
    pallas_call x1, Pallas kernels, body(): pl.pallas_call(functools.partial(sweep_kernel, walls, harms), out_shape=(...  114 us
    pallas_call x1, Pallas kernels, body(): pl.pallas_call(factor_kernel, out_shape=(jax.ShapeDtypeStruct((count, row...  16.4 us
    unnamed x12, local copies, waits for them, and re-layouts  6.19 us

profile of v1, /device:TPU:0, one launch (start us, length us, event | category | flops | bytes accessed | tf_op | source)
XLA Modules:
  0.0 137.4 jit_solution(13977030992293957549)
XLA Ops:
  0.6 0.0 copy-start
  0.6 1.6 %copy-done = bf16[4,256,1024]{2,1,0:T(8,128)(2,1)S(1)} copy-done((bf16[4,256,1024]{2,1,0:T(8,128)(2,1)S(1)}, bf16[4,256,1024]{2,1,0:T(8,128)(2,1)}, u32[]{:S(2)}) %copy-start) | copy-done | bytes 2097176
  2.2 0.0 copy-start.1
  2.2 1.6 %copy-done.1 = bf16[4,256,1024]{2,1,0:T(8,128)(2,1)S(1)} copy-done((bf16[4,256,1024]{2,1,0:T(8,128)(2,1)S(1)}, bf16[4,256,1024]{2,1,0:T(8,128)(2,1)}, u32[]{:S(2)}) %copy-start.1) | copy-done | bytes 2097176
  3.8 0.0 copy-start.3
  3.8 0.9 copy-done.3
  4.8 0.0 copy-start.5
  4.8 0.7 copy-done.5
  5.4 114.2 %sweeps.1 = (f32[4,256,128]{2,1,0:T(8,128)S(1)}, f32[128,128]{1,0:T(8,128)S(1)}) custom-call(s32[4]{0:T(128)S(1)} %copy-done.5, bf16[4,256,128]{2,1,0:T(8,128)(2,1)S(1)} %copy-done.3, bf16[4,256,1024]{2,1,0:T(8,128)(2,1)S(1)} %copy-done, bf16[4,256,1024]{2,1,0:T(8,128)(2,1)S(1)} %copy-done.1, bf16[4,256,1024]{2,1,0:T(8,128)(2,1)} %down.1), custom_call_target="tpu_custom_call" | custom-call | tf_op jit(solution)/shard_map/sweeps/pallas_call | solution.py:261
  119.6 0.0 copy-start.2
  119.6 0.8 copy-done.2
  120.4 0.0 copy-start.4
  120.4 0.6 copy-done.4
  121.1 16.4 %factor.1 = (f32[4,256,128]{2,1,0:T(8,128)}, f32[128,128]{1,0:T(8,128)}) custom-call(f32[4,256,128]{2,1,0:T(8,128)} %copy-done.2, f32[128,128]{1,0:T(8,128)} %copy-done.4), custom_call_target="tpu_custom_call" | custom-call | tf_op jit(solution)/shard_map/factor/pallas_call | solution.py:292
Async XLA Ops:
  0.6 1.6 %copy-start = (bf16[4,256,1024]{2,1,0:T(8,128)(2,1)S(1)}, bf16[4,256,1024]{2,1,0:T(8,128)(2,1)}, u32[]{:S(2)}) copy-start(bf16[4,256,1024]{2,1,0:T(8,128)(2,1)} %inverse.1) | copy-start | bytes 6291460
  2.2 1.6 %copy-start.1 = (bf16[4,256,1024]{2,1,0:T(8,128)(2,1)S(1)}, bf16[4,256,1024]{2,1,0:T(8,128)(2,1)}, u32[]{:S(2)}) copy-start(bf16[4,256,1024]{2,1,0:T(8,128)(2,1)} %up.1) | copy-start | bytes 6291460
  3.8 0.9 copy-start.3
  4.8 0.7 copy-start.5
  119.6 0.8 copy-start.2
  120.4 0.6 copy-start.4

commit v2 on v1

--- a/solution.py
+++ b/solution.py
@@ -29,7 +29,8 @@
 
 def sweep_kernel(
     walls, harms, strip, sketch, inverse, up, down, sampled, gram,
-    pieces, inverse_v, couple_v, products, partial, halo_out, halo_in, gram_out, gram_in,
+    pieces, inverse_v, couple_v, products, partial, halo_out, halo_in,
+    whole, summed, gathered, gram_out, gram_in,
     load_sem, recv_sem, send_sem, halo_send, halo_recv, gram_send, gram_recv,
 ):
     count, rows, width = sketch.shape
@@ -39,8 +40,12 @@
     wall_bits, harm_bits = bits_of(walls), bits_of(harms)
     order = visit_order(count)
 
+    near = min(4, harms)
+    butterfly = [("wall", flip(w, b)) for b in wall_bits if b > 1]
+    butterfly += [("harm", flip(z, b)) for b in harm_bits if b >= near]
     greet = [{"wall": flip(w, b)} for b in wall_bits]
-    greet += [{"harm": flip(z, b)} for b in harm_bits]
+    greet += [{"harm": flip(z, b)} for b in harm_bits if b >= near]
+    greet += [{"harm": z - z % near + (z % near + d) % near} for d in range(1, near)]
     greet += [{"harm": prev}, {"harm": following}]
     barrier = pltpu.get_barrier_semaphore()
 
@@ -159,16 +164,19 @@
     for s in range(SWEEPS):
         g_state, g_rhs = 1 + 2 * s, 2 + 2 * s
         done, sent = set(), set()
-        for h in order:
-            collect(g_state, h)
+        for start in range(0, count, 2):
+            group = order[start : start + 2]
+            for h in group:
+                collect(g_state, h)
 
             @pl.loop(0, 2 * BAND)
             def _(j):
-                products[j, h + BAND] = jnp.dot(
-                    couple_v[j], pieces[g_state, h], preferred_element_type=jnp.float32
-                )
-
-            done.add(h)
+                state = jnp.concatenate([pieces[g_state, h] for h in group], axis=1)
+                both = jnp.dot(couple_v[j], state, preferred_element_type=jnp.float32)
+                for at, h in enumerate(group):
+                    products[j, h + BAND] = both[:, at * width : (at + 1) * width]
+
+            done |= set(group)
             for side, i, need in slots:
                 if (side, i) not in sent and need <= done:
                     sent.add((side, i))
@@ -208,40 +216,86 @@
                     precision=lax.Precision.HIGHEST, preferred_element_type=jnp.float32,
                 )
 
-    stages = [("wall", flip(w, b)) for b in wall_bits] + [("harm", flip(z, b)) for b in harm_bits]
-    for stage, (axis, peer) in enumerate(stages):
-        gram_out[stage] = total
-        swap = pltpu.make_async_remote_copy(
-            src_ref=gram_out.at[stage], dst_ref=gram_in.at[stage],
-            send_sem=gram_send.at[stage], recv_sem=gram_recv.at[stage],
-            device_id={axis: peer}, device_id_type=MESH,
-        )
-        swap.start()
-        swap.wait()
-        total = total + gram_in[stage]
-    gram[...] = total / (harms * walls * count * rows)
+    part = width // 2
+    mine, theirs = (w % 2) * part, (1 - w % 2) * part
+
+    def swap(stage, source, target, peer):
+        copy = pltpu.make_async_remote_copy(
+            src_ref=source, dst_ref=target, send_sem=gram_send.at[stage],
+            recv_sem=gram_recv.at[stage], device_id=peer, device_id_type=MESH,
+        )
+        copy.start()
+        return copy
+
+    whole[...] = total
+    swap(
+        0, whole.at[pl.ds(pl.multiple_of(theirs, part), part)], gram_in.at[0], {"wall": flip(w, 1)}
+    ).wait()
+    half = whole[pl.ds(pl.multiple_of(mine, part), part), :] + gram_in[0]
+    stage = 1
+    for axis, peer in butterfly:
+        gram_out[stage] = half
+        swap(stage, gram_out.at[stage], gram_in.at[stage], {axis: peer}).wait()
+        half = half + gram_in[stage]
+        stage += 1
+    me = z % near
+    gathered[me] = half
+    copies = [
+        swap(stage + d - 1, gathered.at[me], gathered.at[me], {"harm": z - me + (me + d) % near})
+        for d in range(1, near)
+    ]
+    for copy in copies:
+        copy.wait()
+    half = gathered[0]
+    for d in range(1, near):
+        half = half + gathered[d]
+    stage += near - 1
+    half = half / (harms * walls * count * rows)
+    place = pl.ds(pl.multiple_of(mine, part), part)
+    summed[place, :] = half
+    swap(stage, summed.at[place], summed.at[place], {"wall": flip(w, 1)}).wait()
+    gram[...] = summed[...]
 
 
 def factor_kernel(sampled, gram, basis, triangle, work, inverse_lower):
     count, rows, width = sampled.shape
+    panel = 8
     row_at = lax.broadcasted_iota(jnp.int32, (width, width), 0)
     col_at = lax.broadcasted_iota(jnp.int32, (width, width), 1)
+    at = lax.broadcasted_iota(jnp.int32, (panel, width), 0)
     work[...] = gram[...]
     inverse_lower[...] = jnp.where(row_at == col_at, 1.0, 0.0)
 
-    @pl.loop(0, width)
-    def _(k):
-        a = work[...]
-        x = inverse_lower[...]
-        row = work[pl.ds(k, 1), :]
-        x_row = inverse_lower[pl.ds(k, 1), :]
-        column = jnp.sum(jnp.where(col_at == k, a, 0.0), axis=1, keepdims=True)
-        pivot = jnp.sum(jnp.where(col_at[:1] == k, row, 0.0), axis=1, keepdims=True)
-        unit = lax.rsqrt(pivot)
-        factor = jnp.where(row_at[:, :1] > k, column / pivot, 0.0)
-        here = row_at == k
-        work[...] = jnp.where(here, row * unit, a - factor * row)
-        inverse_lower[...] = jnp.where(here, x_row * unit, x - factor * x_row)
+    def spread(value, i):
+        return jnp.broadcast_to(value[i : i + 1, :], (panel, width))
+
+    for low in range(0, width, panel):
+        a = work[low : low + panel, :]
+        x = inverse_lower[low : low + panel, :]
+        columns = [
+            jnp.broadcast_to(a[:, low + i : low + i + 1], (panel, width)) for i in range(panel)
+        ]
+        pivots = jnp.ones((panel, width), jnp.float32)
+        for i in range(panel):
+            pivot = spread(columns[i], i)
+            pivots = jnp.where(at == i, pivot, pivots)
+            factor = jnp.where(at > i, columns[i] * (1.0 / pivot), 0.0)
+            for m in range(i + 1, panel):
+                columns[m] = columns[m] - factor * spread(columns[m], i)
+            a = a - factor * spread(a, i)
+            x = x - factor * spread(x, i)
+        unit = lax.rsqrt(pivots)
+        a, x = a * unit, x * unit
+        work[low : low + panel, :] = a
+        inverse_lower[low : low + panel, :] = x
+        if low + panel < width:
+            change = lax.dot_general(
+                a, jnp.concatenate([a, x], axis=1), (((0,), (0,)), ((), ())),
+                precision=lax.Precision.HIGHEST, preferred_element_type=jnp.float32,
+            )
+            below = low + panel
+            work[below:, :] = work[below:, :] - change[below:, :width]
+            inverse_lower[below:, :] = inverse_lower[below:, :] - change[below:, width:]
 
     triangle[...] = jnp.where(row_at <= col_at, work[...], 0.0)
     for h in range(count):
@@ -254,7 +308,8 @@
 def body(walls, harms, sketch, inverse_blocks, couple_up, couple_down, strip_harmonics):
     count, rows, width = sketch.shape
     size = rows * walls
-    wall_hops, stages = len(bits_of(walls)), len(bits_of(walls)) + len(bits_of(harms))
+    near = min(4, harms)
+    stages = len(bits_of(walls)) + len(bits_of(harms // near)) + near
     gathers = 1 + 2 * SWEEPS
     vmem = pl.BlockSpec(memory_space=pltpu.VMEM)
     anywhere = pl.BlockSpec(memory_space=pl.ANY)
@@ -274,8 +329,11 @@
             pltpu.VMEM((count, rows, width), jnp.float32),
             pltpu.VMEM((SWEEPS, 2, BAND, rows, width), jnp.bfloat16),
             pltpu.VMEM((SWEEPS, 2, BAND, rows, width), jnp.bfloat16),
-            pltpu.VMEM((stages, width, width), jnp.float32),
-            pltpu.VMEM((stages, width, width), jnp.float32),
+            pltpu.VMEM((width, width), jnp.float32),
+            pltpu.VMEM((width, width), jnp.float32),
+            pltpu.VMEM((near, width // 2, width), jnp.float32),
+            pltpu.VMEM((stages, width // 2, width), jnp.float32),
+            pltpu.VMEM((stages, width // 2, width), jnp.float32),
             pltpu.SemaphoreType.DMA((2 * count + 2,)),
             pltpu.SemaphoreType.DMA((gathers, count, walls)),
             pltpu.SemaphoreType.DMA((count, walls)),
@@ -285,7 +343,7 @@
             pltpu.SemaphoreType.DMA((stages,)),
         ],
         compiler_params=pltpu.CompilerParams(
-            collective_id=0, has_side_effects=True, vmem_limit_bytes=48 * 1024 * 1024
+            collective_id=0, has_side_effects=True, vmem_limit_bytes=67043328
         ),
         name="sweeps",
     )(strip_harmonics, sketch, inverse_blocks, couple_up, couple_down)

time: 138 us -> 118 us (0.86)
  Pallas kernels: 131 us -> 118 us
  local copies, waits for them, and re-layouts: 6.19 us -> 0 us
    pallas_call x1, Pallas kernels: 114 us -> 107 us  [body(): pl.pallas_call(functools.partial(sweep_kernel, walls, harms), out_shape=(...]
    unnamed x12 -> x0, local copies, waits for them, and re-layouts: 6.19 us -> none
    pallas_call x1, Pallas kernels: 16.4 us -> 10.9 us  [body(): pl.pallas_call(factor_kernel, out_shape=(jax.ShapeDtypeStruct((count, row...]
where the time goes in v2:
time: 118 us
  Pallas kernels  118 us (100%)
    pallas_call x1, Pallas kernels, body(): pl.pallas_call(functools.partial(sweep_kernel, walls, harms), out_shape=(...  107 us
    pallas_call x1, Pallas kernels, body(): pl.pallas_call(factor_kernel, out_shape=(jax.ShapeDtypeStruct((count, row...  10.9 us

profile of v2, /device:TPU:0, one launch (start us, length us, event | category | flops | bytes accessed | tf_op | source)
XLA Modules:
  0.0 118.3 jit_solution(16806655447828071846)
XLA Ops:
  0.6 106.8 %sweeps.1 = (f32[4,256,128]{2,1,0:T(8,128)}, f32[128,128]{1,0:T(8,128)}) custom-call(s32[4]{0:T(128)} %strip.1, bf16[4,256,128]{2,1,0:T(8,128)(2,1)} %sketch.1, bf16[4,256,1024]{2,1,0:T(8,128)(2,1)} %inverse.1, bf16[4,256,1024]{2,1,0:T(8,128)(2,1)} %up.1, bf16[4,256,1024]{2,1,0:T(8,128)(2,1)} %down.1), custom_call_target="tpu_custom_call" | custom-call | tf_op jit(solution)/shard_map/sweeps/pallas_call | solution.py:316
  107.5 10.9 %factor.1 = (f32[4,256,128]{2,1,0:T(8,128)}, f32[128,128]{1,0:T(8,128)}) custom-call(f32[4,256,128]{2,1,0:T(8,128)} %get-tuple-element.4.sampled, f32[128,128]{1,0:T(8,128)} %get-tuple-element.5.gram), custom_call_target="tpu_custom_call" | custom-call | tf_op jit(solution)/shard_map/factor/pallas_call | solution.py:350

commit v3 on v2

--- a/solution.py
+++ b/solution.py
@@ -95,12 +95,20 @@
         for bit in reversed(wall_bits):
             hop(g, h, 0, bit).start()
 
-    def collect(g, h):
-        for m in sorted(range(1, walls), key=lambda m: -(m & -m)):
+    def relay(g, h):
+        for m in sorted(range(2, walls, 2), key=lambda m: -(m & -m)):
             arrival(g, h, m).wait_recv()
             for bit in reversed(wall_bits):
                 if bit < (m & -m):
                     hop(g, h, m, bit).start()
+
+    def finish(g, h):
+        for m in range(1, walls, 2):
+            arrival(g, h, m).wait_recv()
+
+    def collect(g, h):
+        relay(g, h)
+        finish(g, h)
 
     def settle(g, h):
         for m in range(1, walls):
@@ -165,17 +173,23 @@
         g_state, g_rhs = 1 + 2 * s, 2 + 2 * s
         done, sent = set(), set()
         for start in range(0, count, 2):
-            group = order[start : start + 2]
+            group, later = order[start : start + 2], order[start + 2 : start + 4]
             for h in group:
-                collect(g_state, h)
-
-            @pl.loop(0, 2 * BAND)
-            def _(j):
+                if start == 0:
+                    relay(g_state, h)
+            for h in group:
+                finish(g_state, h)
+
+            def couple(j):
                 state = jnp.concatenate([pieces[g_state, h] for h in group], axis=1)
                 both = jnp.dot(couple_v[j], state, preferred_element_type=jnp.float32)
                 for at, h in enumerate(group):
                     products[j, h + BAND] = both[:, at * width : (at + 1) * width]
 
+            pl.loop(0, BAND, unroll=BAND)(couple)
+            for h in later:
+                relay(g_state, h)
+            pl.loop(BAND, 2 * BAND, unroll=BAND)(couple)
             done |= set(group)
             for side, i, need in slots:
                 if (side, i) not in sent and need <= done:

time: 118 us -> 110 us (0.932)
  Pallas kernels: 118 us -> 109 us
    pallas_call x1, Pallas kernels: 107 us -> 98.5 us  [body(): pl.pallas_call(functools.partial(sweep_kernel, walls, harms), out_shape=(...]
where the time goes in v3:
time: 110 us
  Pallas kernels  109 us (99%)
    pallas_call x1, Pallas kernels, body(): pl.pallas_call(functools.partial(sweep_kernel, walls, harms), out_shape=(...  98.5 us
    pallas_call x1, Pallas kernels, body(): pl.pallas_call(factor_kernel, out_shape=(jax.ShapeDtypeStruct((count, row...  10.9 us

profile of v3, /device:TPU:0, one launch (start us, length us, event | category | flops | bytes accessed | tf_op | source)
XLA Modules:
  0.0 110.0 jit_solution(13791115353017443071)
XLA Ops:
  0.6 98.5 %sweeps.1 = (f32[4,256,128]{2,1,0:T(8,128)}, f32[128,128]{1,0:T(8,128)}) custom-call(s32[4]{0:T(128)} %strip.1, bf16[4,256,128]{2,1,0:T(8,128)(2,1)} %sketch.1, bf16[4,256,1024]{2,1,0:T(8,128)(2,1)} %inverse.1, bf16[4,256,1024]{2,1,0:T(8,128)(2,1)} %up.1, bf16[4,256,1024]{2,1,0:T(8,128)(2,1)} %down.1), custom_call_target="tpu_custom_call" | custom-call | tf_op jit(solution)/shard_map/sweeps/pallas_call | solution.py:330
  99.1 10.9 %factor.1 = (f32[4,256,128]{2,1,0:T(8,128)}, f32[128,128]{1,0:T(8,128)}) custom-call(f32[4,256,128]{2,1,0:T(8,128)} %get-tuple-element.4.sampled, f32[128,128]{1,0:T(8,128)} %get-tuple-element.5.gram), custom_call_target="tpu_custom_call" | custom-call | tf_op jit(solution)/shard_map/factor/pallas_call | solution.py:364
